TPU v7x, 32 devices: a whole 2x2x4 slice. The times are simulated.
32 devices in a mesh: orb: 4 (over z), tile: 8 (over y, x, core).
Axes of the slice: x: 2, y: 2, z: 4, core: 2. Of those that a mesh axis runs over, the one named last changes fastest.
Arguments:
- basis_values: bfloat16 [2048, 65536], P('tile'), may hold values from -6 to 6
- coefficients: bfloat16 [65536, 128], P('tile', 'orb'), may hold values from -0.03125 to 0.03125
- occupations: float32 [128], P('orb'), may hold values from 0.5 to 2
- owners: int32 [2048, 1], P('tile'), may hold values from 0 to 7; in each aligned block of 256 rows (0 to 255, 256 to 511, ...) at most 64 rows name the same one
- offsets: int32 [2048], P('tile'), may hold values from 0 to 8191
Outputs:
- density: float32 [64, 64, 128], P('tile', 'orb')
- gradient: float32 [3, 64, 64, 128], P(None, 'tile', 'orb')
Inputs may be any that keep to these rules, and one draw needn't show every extreme that they name: `owners`: at most 64 entries of one tile's list name the same owner, and some tile's list reaches 64.
All inputs are finite; a program needn't handle non-finite values.
Results may differ from a plain program's by a relative error of at most 0.0003.
Values may be sent and summed in bfloat16 or wider, within the bound.
A program may use at most 320 MiB of HBM per device.

v0:
```python
import jax
import jax.numpy as jnp
from jax import lax
from jax.sharding import PartitionSpec as P

CY = 64
CZ = 128


def with_halo(cells, sides, width):
    for axis, dim in sides:
        count = lax.axis_size(axis)
        ends = count - 1
        head = lax.slice_in_dim(cells, 0, width, axis=dim)
        tail = lax.slice_in_dim(cells, cells.shape[dim] - width, cells.shape[dim], axis=dim)
        cells = jnp.concatenate(
            [
                lax.ppermute(tail, axis, [(i, (i + 1) % count) for i in range(ends)]),
                cells,
                lax.ppermute(head, axis, [((i + 1) % count, i) for i in range(ends)]),
            ],
            axis=dim,
        )
    return cells


def central(padded):
    along_x = 0.5 * (padded[2:, 1:-1, 1:-1] - padded[:-2, 1:-1, 1:-1])
    along_y = 0.5 * (padded[1:-1, 2:, 1:-1] - padded[1:-1, :-2, 1:-1])
    along_z = 0.5 * (padded[1:-1, 1:-1, 2:] - padded[1:-1, 1:-1, :-2])
    return jnp.stack([along_x, along_y, along_z])


def body(basis_values, coefficients, occupations, owners, offsets):
    listed_count = owners.shape[0]
    rows_held = coefficients.shape[0]
    local_orbitals = coefficients.shape[1]
    owner_ids = owners[:, 0]
    global_rows = owner_ids * rows_held + offsets
    empty = jnp.zeros((listed_count, local_orbitals), jnp.bfloat16)
    shard_rows = lax.all_gather(coefficients, "tile", axis=0, tiled=True)
    inside = (global_rows >= 0) & (global_rows < shard_rows.shape[0])
    safe_rows = jnp.clip(global_rows, 0, shard_rows.shape[0] - 1)
    taken = jnp.take(shard_rows, safe_rows, axis=0)
    listed = jnp.where(inside[:, None], taken, empty)
    depth_cells = basis_values.shape[1] // (CY * CZ)
    share_width = CY // lax.axis_size("orb")
    orbitals = jnp.einsum("bo,bc->oc", listed, basis_values, preferred_element_type=jnp.float32)
    partial_value = jnp.sum(occupations[:, None] * orbitals * orbitals, axis=0).reshape(
        depth_cells, CY, CZ
    )
    density_full = lax.psum(partial_value, "orb")
    padded = with_halo(density_full, (("tile", 0),), 1)
    padded = jnp.pad(padded, ((0, 0), (1, 1), (1, 1)))
    first_col = lax.axis_index("orb") * share_width
    density = lax.dynamic_slice_in_dim(density_full, first_col, share_width, 1)
    gradient = lax.dynamic_slice_in_dim(central(padded), first_col, share_width, 2)
    return (density, gradient)


def solution(mesh):
    placed = (P("tile", None), P("tile", "orb"), P("orb"), P("tile", None), P("tile"))
    return jax.shard_map(
        body,
        mesh=mesh,
        in_specs=placed,
        out_specs=(P("tile", "orb", None), P(None, "tile", "orb", None)),
        check_vma=False,
    )
```

profile of v0, /device:TPU:4, one launch (start us, length us, event | category | flops | bytes accessed | tf_op | source)
XLA Modules:
  0.0 181.8 jit_solution(3366293693858491619)
XLA Ops:
  7.2 0.0 all-gather.2.cloned.1.call-start
  7.2 2.7 %copy.7 = bf16[8192,32]{1,0:T(8,128)(2,1)} copy(bf16[8192,32]{0,1:T(8,128)(2,1)} %param.6) | data formatting | bytes 1048576 | tf_op args[1]
  9.9 0.0 all-gather.2.cloned.1.call-update
  9.9 0.0 all-reduce.3.cloned.1.call-start
  10.0 0.7 broadcast_multiply_fusion
  10.6 0.7 compare_and_fusion
  11.3 88.9 %all-gather.2.cloned.1.call-done = bf16[65536,32]{1,0:T(8,128)(2,1)} async-done(((bf16[8192,32]{1,0:T(8,128)(2,1)}), bf16[65536,32]{1,0:T(8,128)(2,1)}) %all-gather.2.cloned.1.call-update) | async-done | bytes 4194320 | tf_op jit(solution)/shard_map/all_gather | solution.py:41
  100.3 8.7 %gather_fusion = bf16[256,32]{1,0:T(8,128)(2,1)S(1)} fusion(bf16[65536,32]{1,0:T(8,128)(2,1)} %all-gather.2.cloned.1.call-done, s32[1024]{0:T(1024)S(1)} %pad_clamp_fusion), kind=kCustom, calls=%fused_computation | custom fusion | bytes 33792 | tf_op jit(solution)/shard_map/jit(_take)/gather | solution.py:44
  108.9 17.4 %fusion = f32[65536]{0:T(1024)} fusion(f32[32]{0:T(128)} %param.7, bf16[256,65536]{1,0:T(8,128)(2,1)} %param.5, bf16[256,32]{1,0:T(8,128)(2,1)S(1)} %gather_fusion, pred[256]{0:T(512)(128)(4,1)S(1)} %get-tuple-element.2, pred[256]{0:T(512)(128)(4,1)S(1)} %get-tuple-element.8), kind=kOutput, calls=%fused_computation.2 | convolution fusion | flops 1079984128 | bytes 33833600 | tf_op jit(solution)/shard_map/bo,bc->oc/dot_general | solution.py:48
  126.3 0.0 all-reduce.3.cloned.1.call-update
  126.4 36.5 %all-reduce.3.cloned.1.call-done = f32[8,64,128]{2,1,0:T(8,128)} async-done(((f32[8,64,128]{2,1,0:T(8,128)}), f32[8,64,128]{2,1,0:T(8,128)}) %all-reduce.3.cloned.1.call-update) | async-done | bytes 262160 | tf_op jit(solution)/shard_map/psum | solution.py:52
  162.8 0.8 fusion.24
  163.6 1.9 %collective-permute-start = (f32[1,64,128]{2,1,0:T(8,128)S(1)}, f32[1,64,128]{2,1,0:T(8,128)S(1)}, u32[]{:S(2)}, u32[]{:S(2)}) collective-permute-start(f32[1,64,128]{2,1,0:T(8,128)S(1)} %get-tuple-element.6), channel_id=1, source_target_pairs={{1,0},{2,1},{3,2},{4,3},{5,4},{6,5},{7,6},{9,8},{10,9},{11,10},{12... | collective-permute-start | bytes 98312 | tf_op jit(solution)/shard_map/ppermute | solution.py:20
  165.5 2.4 %collective-permute-start.1 = (f32[1,64,128]{2,1,0:T(8,128)S(1)}, f32[1,64,128]{2,1,0:T(8,128)S(1)}, u32[]{:S(2)}, u32[]{:S(2)}) collective-permute-start(f32[1,64,128]{2,1,0:T(8,128)S(1)} %get-tuple-element.7), channel_id=1, source_target_pairs={{0,1},{1,2},{2,3},{3,4},{4,5},{5,6},{6,7},{8,9},{9,10},{10,11},{11... | collective-permute-start | bytes 98312 | tf_op jit(solution)/shard_map/ppermute | solution.py:18
  167.9 1.5 constant_dynamic-slice_fusion
  169.4 0.0 collective-permute-done
  169.4 2.2 %collective-permute-done.1 = f32[1,64,128]{2,1,0:T(8,128)S(1)} collective-permute-done((f32[1,64,128]{2,1,0:T(8,128)S(1)}, f32[1,64,128]{2,1,0:T(8,128)S(1)}, u32[]{:S(2)}, u32[]{:S(2)}) %collective-permute-start.1) | collective-permute-done | bytes 32800 | tf_op jit(solution)/shard_map/ppermute | solution.py:18
  171.7 1.2 select_maximum_fusion
  172.9 1.3 fusion.5
  174.2 0.7 fusion.12
  (1 shorter events, 0.0 us)
Async XLA Ops:
  7.2 93.1 %all-gather.2.cloned.1.call-start = ((), (), s32[]{:S(2)}) async-start(), calls=%async_computation | async-start | bytes 18874368 | tf_op jit(solution)/shard_map/all_gather | solution.py:41
  9.9 152.9 %all-reduce.3.cloned.1.call-start = ((), (), s32[]{:S(2)}) async-start(), calls=%async_computation.1 | async-start | bytes 524288 | tf_op jit(solution)/shard_map/psum | solution.py:52
  163.6 5.8 %collective-permute-start = (f32[1,64,128]{2,1,0:T(8,128)S(1)}, f32[1,64,128]{2,1,0:T(8,128)S(1)}, u32[]{:S(2)}, u32[]{:S(2)}) collective-permute-start(f32[1,64,128]{2,1,0:T(8,128)S(1)} %get-tuple-element.6), channel_id=1, source_target_pairs={{1,0},{2,1},{3,2},{4,3},{5,4},{6,5},{7,6},{9,8},{10,9},{11,10},{12... | collective-permute-start | bytes 98312 | tf_op jit(solution)/shard_map/ppermute | solution.py:20
  165.5 6.1 %collective-permute-start.1 = (f32[1,64,128]{2,1,0:T(8,128)S(1)}, f32[1,64,128]{2,1,0:T(8,128)S(1)}, u32[]{:S(2)}, u32[]{:S(2)}) collective-permute-start(f32[1,64,128]{2,1,0:T(8,128)S(1)} %get-tuple-element.7), channel_id=1, source_target_pairs={{0,1},{1,2},{2,3},{3,4},{4,5},{5,6},{6,7},{8,9},{9,10},{10,11},{11... | collective-permute-start | bytes 98312 | tf_op jit(solution)/shard_map/ppermute | solution.py:18
Sparse Core Ops, SparseCore 0:
  10.0 90.1 all-gather.1
  126.5 36.3 all-reduce.2
where the time goes:
time: 182 us
  waiting for transfers between devices  128 us (70%)
  matrix products  17.4 us (10%)
  between operations  14.1 us (8%)
  local copies, waits for them, and re-layouts  13.6 us (7%)
  other arithmetic  4.62 us (3%)
  starting transfers between devices  4.39 us (2%)
    all_gather x1, waiting for transfers between devices, body(): shard_rows = lax.all_gather(coefficients, 'tile', axis=0, tiled=True)  88.9 us
    psum x1, waiting for transfers between devices, body(): density_full = lax.psum(partial_value, 'orb')  36.5 us
    dot_general x1, matrix products, body(): jnp.einsum('bo,bc->oc', listed, basis_values, preferred_element_type=jnp....  17.4 us
    gather x1, local copies, waits for them, and re-layouts, body(): taken = jnp.take(shard_rows, safe_rows, axis=0)  8.65 us
  transfers between devices with their start and end apart: 4, of which 3 were waited for; matrix products, arithmetic and copies ran while one was open for 2% of the time, Pallas kernels for 0%

commit v1 on v0

--- a/solution.py
+++ b/solution.py
@@ -38,7 +38,12 @@
     owner_ids = owners[:, 0]
     global_rows = owner_ids * rows_held + offsets
     empty = jnp.zeros((listed_count, local_orbitals), jnp.bfloat16)
-    shard_rows = lax.all_gather(coefficients, "tile", axis=0, tiled=True)
+    ring = [coefficients]
+    for hop in range(7):
+        ring.append(lax.ppermute(ring[-1], "tile", [(dev, (dev + 1) % 8) for dev in range(8)]))
+    shard_rows = jnp.roll(
+        jnp.concatenate(ring[::-1], axis=0), (lax.axis_index("tile") + 1) * ring[0].shape[0], axis=0
+    )
     inside = (global_rows >= 0) & (global_rows < shard_rows.shape[0])
     safe_rows = jnp.clip(global_rows, 0, shard_rows.shape[0] - 1)
     taken = jnp.take(shard_rows, safe_rows, axis=0)

time: 182 us -> 176 us (0.967)
  waiting for transfers between devices: 128 us -> 104 us
  local copies, waits for them, and re-layouts: 13.6 us -> 30.5 us
    all_gather x1 -> x0, waiting for transfers between devices: 88.9 us -> none  [body(): shard_rows = lax.all_gather(coefficients, 'tile', axis=0, tiled=True)]
    ppermute x0 -> x7, waiting for transfers between devices: none -> 65.6 us  [body(): lax.ppermute(ring[-1], 'tile', [(dev, (dev + 1) % 8) for dev in range(8)])]
    unnamed x1 -> x20, local copies, waits for them, and re-layouts: 2.68 us -> 17.3 us
    dynamic_slice x0 -> x1, local copies, waits for them, and re-layouts: none -> 2.23 us  [body(): jnp.roll(jnp.concatenate(ring[::-1], axis=0), (lax.axis_index('tile') + 1...]
  transfers between devices with their start and end apart: 4 -> 10, of which waited for: 3 -> 9; matrix products, arithmetic and copies ran while one was open for 2% -> 2% of each run, Pallas kernels for 0% -> 0%
where the time goes in v1:
time: 176 us; the launch traced here: 175 us
  waiting for transfers between devices  104 us (59%)
  local copies, waits for them, and re-layouts  30.5 us (17%)
  matrix products  17.4 us (10%)
  between operations  14.2 us (8%)
  other arithmetic  4.62 us (3%)
  starting transfers between devices  4.43 us (3%)
    ppermute x7, waiting for transfers between devices, body(): lax.ppermute(ring[-1], 'tile', [(dev, (dev + 1) % 8) for dev in range(8)])  65.6 us
    psum x1, waiting for transfers between devices, body(): density_full = lax.psum(partial_value, 'orb')  36 us
    dot_general x1, matrix products, body(): jnp.einsum('bo,bc->oc', listed, basis_values, preferred_element_type=jnp....  17.4 us
    unnamed x20, local copies, waits for them, and re-layouts  17.3 us
    gather x1, local copies, waits for them, and re-layouts, body(): taken = jnp.take(shard_rows, safe_rows, axis=0)  8.65 us
  transfers between devices with their start and end apart: 10, of which 9 were waited for; matrix products, arithmetic and copies ran while one was open for 2% of the time, Pallas kernels for 0%

profile of v1, /device:TPU:4, one launch (start us, length us, event | category | flops | bytes accessed | tf_op | source)
XLA Modules:
  0.0 175.0 jit_solution(17970166220957680762)
XLA Ops:
  7.2 0.0 copy-start
  7.2 0.0 all-reduce.3.cloned.1.call-start
  7.2 0.1 collective-permute-start
  7.3 9.7 %collective-permute-done = bf16[8192,32]{0,1:T(8,128)(2,1)S(1)} collective-permute-done((bf16[8192,32]{0,1:T(8,128)(2,1)}, bf16[8192,32]{0,1:T(8,128)(2,1)S(1)}, u32[]{:S(2)}, u32[]{:S(2)}) %collective-permute-start) | collective-permute-done | bytes 524320 | tf_op jit(solution)/shard_map/ppermute | solution.py:43
  17.0 9.5 %collective-permute-done.1 = bf16[8192,32]{0,1:T(8,128)(2,1)S(1)} collective-permute-done((bf16[8192,32]{0,1:T(8,128)(2,1)S(1)}, bf16[8192,32]{0,1:T(8,128)(2,1)S(1)}, u32[]{:S(2)}, u32[]{:S(2)}) %collective-permute-start.1) | collective-permute-done | bytes 524320 | tf_op jit(solution)/shard_map/ppermute | solution.py:43
  26.5 0.0 collective-permute-start.2
  26.5 9.5 %collective-permute-done.2 = bf16[8192,32]{0,1:T(8,128)(2,1)S(1)} collective-permute-done((bf16[8192,32]{0,1:T(8,128)(2,1)S(1)}, bf16[8192,32]{0,1:T(8,128)(2,1)S(1)}, u32[]{:S(2)}, u32[]{:S(2)}) %collective-permute-start.2) | collective-permute-done | bytes 524320 | tf_op jit(solution)/shard_map/ppermute | solution.py:43
  36.0 9.5 %collective-permute-done.3 = bf16[8192,32]{0,1:T(8,128)(2,1)S(1)} collective-permute-done((bf16[8192,32]{0,1:T(8,128)(2,1)S(1)}, bf16[8192,32]{0,1:T(8,128)(2,1)S(1)}, u32[]{:S(2)}, u32[]{:S(2)}) %collective-permute-start.3) | collective-permute-done | bytes 524320 | tf_op jit(solution)/shard_map/ppermute | solution.py:43
  45.5 0.0 collective-permute-start.4
  45.5 9.5 %collective-permute-done.4 = bf16[8192,32]{0,1:T(8,128)(2,1)S(1)} collective-permute-done((bf16[8192,32]{0,1:T(8,128)(2,1)S(1)}, bf16[8192,32]{0,1:T(8,128)(2,1)S(1)}, u32[]{:S(2)}, u32[]{:S(2)}) %collective-permute-start.4) | collective-permute-done | bytes 524320 | tf_op jit(solution)/shard_map/ppermute | solution.py:43
  55.0 9.6 %collective-permute-done.5 = bf16[8192,32]{0,1:T(8,128)(2,1)} collective-permute-done((bf16[8192,32]{0,1:T(8,128)(2,1)S(1)}, bf16[8192,32]{0,1:T(8,128)(2,1)}, u32[]{:S(2)}, u32[]{:S(2)}) %collective-permute-start.5) | collective-permute-done | bytes 524320 | tf_op jit(solution)/shard_map/ppermute | solution.py:43
  64.6 0.0 collective-permute-start.6
  64.6 0.7 broadcast_multiply_fusion
  65.3 0.7 compare_and_fusion
  66.0 8.3 %collective-permute-done.6 = bf16[8192,32]{0,1:T(8,128)(2,1)S(1)} collective-permute-done((bf16[8192,32]{0,1:T(8,128)(2,1)}, bf16[8192,32]{0,1:T(8,128)(2,1)S(1)}, u32[]{:S(2)}, u32[]{:S(2)}) %collective-permute-start.6) | collective-permute-done | bytes 524320 | tf_op jit(solution)/shard_map/ppermute | solution.py:43
  74.4 1.1 constant_dynamic-update-slice_fusion.14
  75.7 1.1 constant_dynamic-update-slice_fusion.8
  76.8 1.1 constant_dynamic-update-slice_fusion.6
  78.2 2.2 %constant_dynamic-slice_fusion.1 = bf16[65536,32]{0,1:T(8,128)(2,1)} fusion(bf16[131072,32]{0,1:T(8,128)(2,1)S(1)} %constant_dynamic-update-slice_fusion, s32[]{:T(128)S(6)} %select_n.32), kind=kLoop, calls=%fused_computation.56 | loop fusion | bytes 8388612 | tf_op jit(solution)/shard_map/jit(_roll_dynamic)/dynamic_slice | solution.py:44
  80.4 13.6 %copy.11 = bf16[65536,32]{1,0:T(8,128)(2,1)} copy(bf16[65536,32]{0,1:T(8,128)(2,1)} %constant_dynamic-slice_fusion.1) | data formatting | bytes 8388608
  94.0 8.7 %gather_fusion = bf16[256,32]{1,0:T(8,128)(2,1)S(1)} fusion(bf16[65536,32]{1,0:T(8,128)(2,1)} %copy.11, s32[1024]{0:T(1024)S(1)} %pad_clamp_fusion), kind=kCustom, calls=%fused_computation | custom fusion | bytes 33792 | tf_op jit(solution)/shard_map/jit(_take)/gather | solution.py:49
  102.6 17.4 %fusion = f32[65536]{0:T(1024)} fusion(f32[32]{0:T(128)S(1)} %copy-done.1, bf16[256,65536]{1,0:T(8,128)(2,1)} %param.5, bf16[256,32]{1,0:T(8,128)(2,1)S(1)} %gather_fusion, pred[256]{0:T(512)(128)(4,1)S(1)} %get-tuple-element.2, pred[256]{0:T(512)(128)(4,1)S(1)} %get-tuple-element.8), kind=kOutput, calls=%fused_computation.2 | convolution fusion | flops 1079984128 | bytes 33833600 | tf_op jit(solution)/shard_map/bo,bc->oc/dot_general | solution.py:53
  120.1 0.0 all-reduce.3.cloned.1.call-update
  120.1 36.0 %all-reduce.3.cloned.1.call-done = f32[8,64,128]{2,1,0:T(8,128)} async-done(((f32[8,64,128]{2,1,0:T(8,128)}), f32[8,64,128]{2,1,0:T(8,128)}) %all-reduce.3.cloned.1.call-update) | async-done | bytes 262160 | tf_op jit(solution)/shard_map/psum | solution.py:57
  156.1 0.8 fusion.24
  156.9 1.9 %collective-permute-start.7 = (f32[1,64,128]{2,1,0:T(8,128)S(1)}, f32[1,64,128]{2,1,0:T(8,128)S(1)}, u32[]{:S(2)}, u32[]{:S(2)}) collective-permute-start(f32[1,64,128]{2,1,0:T(8,128)S(1)} %get-tuple-element.6), channel_id=1, source_target_pairs={{1,0},{2,1},{3,2},{4,3},{5,4},{6,5},{7,6},{9,8},{10,9},{11,10},{12... | collective-permute-start | bytes 98312 | tf_op jit(solution)/shard_map/ppermute | solution.py:20
  158.8 2.4 %collective-permute-start.8 = (f32[1,64,128]{2,1,0:T(8,128)S(1)}, f32[1,64,128]{2,1,0:T(8,128)S(1)}, u32[]{:S(2)}, u32[]{:S(2)}) collective-permute-start(f32[1,64,128]{2,1,0:T(8,128)S(1)} %get-tuple-element.7), channel_id=1, source_target_pairs={{0,1},{1,2},{2,3},{3,4},{4,5},{5,6},{6,7},{8,9},{9,10},{10,11},{11... | collective-permute-start | bytes 98312 | tf_op jit(solution)/shard_map/ppermute | solution.py:18
  161.2 1.5 constant_dynamic-slice_fusion
  162.7 2.2 %collective-permute-done.8 = f32[1,64,128]{2,1,0:T(8,128)S(1)} collective-permute-done((f32[1,64,128]{2,1,0:T(8,128)S(1)}, f32[1,64,128]{2,1,0:T(8,128)S(1)}, u32[]{:S(2)}, u32[]{:S(2)}) %collective-permute-start.8) | collective-permute-done | bytes 32800 | tf_op jit(solution)/shard_map/ppermute | solution.py:18
  164.9 1.2 select_maximum_fusion
  166.1 1.3 fusion.5
  167.5 0.7 fusion.12
  (21 shorter events, 0.5 us)
Async XLA Ops:
  7.2 70.9 %copy-start = (bf16[8192,32]{0,1:T(8,128)(2,1)S(1)}, bf16[8192,32]{0,1:T(8,128)(2,1)}, u32[]{:S(2)}) copy-start(bf16[8192,32]{0,1:T(8,128)(2,1)} %param.6) | copy-start | bytes 1572868
  7.2 148.9 %all-reduce.3.cloned.1.call-start = ((), (), s32[]{:S(2)}) async-start(), calls=%async_computation | async-start | bytes 524288 | tf_op jit(solution)/shard_map/psum | solution.py:57
  7.2 9.8 %collective-permute-start = (bf16[8192,32]{0,1:T(8,128)(2,1)}, bf16[8192,32]{0,1:T(8,128)(2,1)S(1)}, u32[]{:S(2)}, u32[]{:S(2)}) collective-permute-start(bf16[8192,32]{0,1:T(8,128)(2,1)} %param.6), channel_id=1, source_target_pairs={{0,1},{1,2},{2,3},{3,4},{4,5},{5,6},{6,7},{7,0},{8,9},{9,10},{10,1... | collective-permute-start | bytes 1572872 | tf_op jit(solution)/shard_map/ppermute | solution.py:43
  17.0 9.5 %collective-permute-start.1 = (bf16[8192,32]{0,1:T(8,128)(2,1)S(1)}, bf16[8192,32]{0,1:T(8,128)(2,1)S(1)}, u32[]{:S(2)}, u32[]{:S(2)}) collective-permute-start(bf16[8192,32]{0,1:T(8,128)(2,1)S(1)} %collective-permute-done), channel_id=1, source_target_pairs={{0,1},{1,2},{2,3},{3,4},{4,5},{5,6},{6,7},{7,0},{8,9},{9,10},{10,1... | collective-permute-start | bytes 1572872 | tf_op jit(solution)/shard_map/ppermute | solution.py:43
  26.5 9.5 %collective-permute-start.2 = (bf16[8192,32]{0,1:T(8,128)(2,1)S(1)}, bf16[8192,32]{0,1:T(8,128)(2,1)S(1)}, u32[]{:S(2)}, u32[]{:S(2)}) collective-permute-start(bf16[8192,32]{0,1:T(8,128)(2,1)S(1)} %collective-permute-done.1), channel_id=1, source_target_pairs={{0,1},{1,2},{2,3},{3,4},{4,5},{5,6},{6,7},{7,0},{8,9},{9,10},{10,1... | collective-permute-start | bytes 1572872 | tf_op jit(solution)/shard_map/ppermute | solution.py:43
  36.0 9.5 %collective-permute-start.3 = (bf16[8192,32]{0,1:T(8,128)(2,1)S(1)}, bf16[8192,32]{0,1:T(8,128)(2,1)S(1)}, u32[]{:S(2)}, u32[]{:S(2)}) collective-permute-start(bf16[8192,32]{0,1:T(8,128)(2,1)S(1)} %collective-permute-done.2), channel_id=1, source_target_pairs={{0,1},{1,2},{2,3},{3,4},{4,5},{5,6},{6,7},{7,0},{8,9},{9,10},{10,1... | collective-permute-start | bytes 1572872 | tf_op jit(solution)/shard_map/ppermute | solution.py:43
  45.5 9.5 %collective-permute-start.4 = (bf16[8192,32]{0,1:T(8,128)(2,1)S(1)}, bf16[8192,32]{0,1:T(8,128)(2,1)S(1)}, u32[]{:S(2)}, u32[]{:S(2)}) collective-permute-start(bf16[8192,32]{0,1:T(8,128)(2,1)S(1)} %collective-permute-done.3), channel_id=1, source_target_pairs={{0,1},{1,2},{2,3},{3,4},{4,5},{5,6},{6,7},{7,0},{8,9},{9,10},{10,1... | collective-permute-start | bytes 1572872 | tf_op jit(solution)/shard_map/ppermute | solution.py:43
  55.0 9.6 %collective-permute-start.5 = (bf16[8192,32]{0,1:T(8,128)(2,1)S(1)}, bf16[8192,32]{0,1:T(8,128)(2,1)}, u32[]{:S(2)}, u32[]{:S(2)}) collective-permute-start(bf16[8192,32]{0,1:T(8,128)(2,1)S(1)} %collective-permute-done.4), channel_id=1, source_target_pairs={{0,1},{1,2},{2,3},{3,4},{4,5},{5,6},{6,7},{7,0},{8,9},{9,10},{10,1... | collective-permute-start | bytes 1572872 | tf_op jit(solution)/shard_map/ppermute | solution.py:43
  64.6 9.7 %collective-permute-start.6 = (bf16[8192,32]{0,1:T(8,128)(2,1)}, bf16[8192,32]{0,1:T(8,128)(2,1)S(1)}, u32[]{:S(2)}, u32[]{:S(2)}) collective-permute-start(bf16[8192,32]{0,1:T(8,128)(2,1)} %collective-permute-done.5), channel_id=1, source_target_pairs={{0,1},{1,2},{2,3},{3,4},{4,5},{5,6},{6,7},{7,0},{8,9},{9,10},{10,1... | collective-permute-start | bytes 1572872 | tf_op jit(solution)/shard_map/ppermute | solution.py:43
  80.4 22.2 %copy-start.1 = (f32[32]{0:T(128)S(1)}, f32[32]{0:T(128)}, u32[]{:S(2)}) copy-start(f32[32]{0:T(128)} %param.7) | copy-start | bytes 388
  156.9 5.8 %collective-permute-start.7 = (f32[1,64,128]{2,1,0:T(8,128)S(1)}, f32[1,64,128]{2,1,0:T(8,128)S(1)}, u32[]{:S(2)}, u32[]{:S(2)}) collective-permute-start(f32[1,64,128]{2,1,0:T(8,128)S(1)} %get-tuple-element.6), channel_id=1, source_target_pairs={{1,0},{2,1},{3,2},{4,3},{5,4},{6,5},{7,6},{9,8},{10,9},{11,10},{12... | collective-permute-start | bytes 98312 | tf_op jit(solution)/shard_map/ppermute | solution.py:20
  158.8 6.1 %collective-permute-start.8 = (f32[1,64,128]{2,1,0:T(8,128)S(1)}, f32[1,64,128]{2,1,0:T(8,128)S(1)}, u32[]{:S(2)}, u32[]{:S(2)}) collective-permute-start(f32[1,64,128]{2,1,0:T(8,128)S(1)} %get-tuple-element.7), channel_id=1, source_target_pairs={{0,1},{1,2},{2,3},{3,4},{4,5},{5,6},{6,7},{8,9},{9,10},{10,11},{11... | collective-permute-start | bytes 98312 | tf_op jit(solution)/shard_map/ppermute | solution.py:18
Sparse Core Ops, SparseCore 0:
  120.2 35.8 all-reduce.2
